TPU v7x, 32 devices: a whole 2x2x4 slice. The times are simulated.
32 devices in a mesh: row: 4 (over y, x), col: 8 (over z, core).
Axes of the slice: x: 2, y: 2, z: 4, core: 2. Of those that a mesh axis runs over, the one named last changes fastest.
Arguments:
- fact_block: int32 [98304, 1], P(('row', 'col')), may hold values from 0 to 31; in each aligned block of 3072 rows (0 to 3071, 3072 to 6143, ...) at most 192 rows name the same one
- fact_offset: int32 [98304], P(('row', 'col')), may hold values from 0 to 2047
- fact_date: int32 [98304], P(('row', 'col')), may hold values from 0 to 2555
- revenue: bfloat16 [98304], P(('row', 'col')), may hold values from 0.5 to 4
- supplier_words: int32 [2208], P('col'), may hold values from 0 to 1073741823
- date_words: int32 [88], P('col'), may hold values from 0 to 1073741823
- candidates: int32 [1024], replicated, may hold values from 0 to 65535
Outputs:
- supplier_revenue: float32 [65536], P(('row', 'col'))
- candidate_revenue: float32 [1024], replicated
- candidate_total: float32 [], replicated
Inputs may be any that keep to these rules, and one draw needn't show every extreme that they name: `fact_block`: each device's rows name no owner block more than 192 times. `candidates`: ids may repeat.
All inputs are finite; a program needn't handle non-finite values.
Results may differ from a plain program's by a relative error of at most 0.0003.
Values sent between devices are 32-bit elements; how exact they have to be, the bound alone decides.
A program may use at most 64 MiB of HBM per device.

v0:
```python
import jax
import jax.numpy as jnp
from jax import lax
from jax.sharding import PartitionSpec as P

SUP_DEV = 2048


def filtered_revenue(owner, fact_offset, fact_date, revenue, supplier_all, date_all):
    words_per_block = (SUP_DEV + 29) // 30
    word_index = owner * words_per_block + fact_offset // 30
    supplier_word = jnp.take(supplier_all, word_index)
    supplier_bit = jnp.bitwise_and(jnp.right_shift(supplier_word, fact_offset % 30), 1)
    date_slot = fact_date // 30
    positions = jnp.arange(date_all.shape[0], dtype=jnp.int32)
    date_word = jnp.sum(
        jnp.where(date_slot[:, None] == positions[None, :], date_all[None, :], 0), axis=1
    )
    date_bit = jnp.bitwise_and(jnp.right_shift(date_word, fact_date % 30), 1)
    return jnp.where(supplier_bit * date_bit == 1, revenue, jnp.zeros_like(revenue))


def per_device(fact_block, fact_offset, fact_date, revenue, supplier_words, date_words, candidates):
    devices = lax.axis_size("row") * lax.axis_size("col")
    supplier_all, date_all = (
        lax.all_gather(supplier_words, "col", axis=0, tiled=True),
        lax.all_gather(date_words, "col", axis=0, tiled=True),
    )
    owner = fact_block[:, 0]
    masked = filtered_revenue(owner, fact_offset, fact_date, revenue, supplier_all, date_all)
    row_count = fact_offset.shape[0]
    capacity = max(2, 2 * row_count // devices)
    row_ids = jnp.arange(row_count, dtype=jnp.int32)
    earlier = (owner[:, None] == owner[None, :]) & (row_ids[None, :] < row_ids[:, None])
    ranking = jnp.sum(earlier, axis=1, dtype=jnp.int32)
    slot_index = owner * capacity + ranking
    slot_revenue = (
        jnp.zeros((devices * capacity,), jnp.float32).at[slot_index].set(masked.astype(jnp.float32))
    )
    slot_offset = (
        jnp.zeros((devices * capacity,), jnp.float32)
        .at[slot_index]
        .set(fact_offset.astype(jnp.float32))
    )
    payload = jnp.stack((slot_revenue, slot_offset), axis=-1)
    payload = payload.reshape(lax.axis_size("row"), lax.axis_size("col"), 2 * capacity)
    arrived = lax.all_to_all(
        lax.all_to_all(payload, "row", split_axis=0, concat_axis=0, tiled=True),
        "col",
        split_axis=1,
        concat_axis=1,
        tiled=True,
    )
    arrived = arrived.reshape(-1, 2)
    owned = jax.ops.segment_sum(
        arrived[:, 0], arrived[:, 1].astype(jnp.int32), num_segments=SUP_DEV
    )
    global_id = owner * SUP_DEV + fact_offset
    onehot_cands = (global_id[:, None] == candidates[None, :]).astype(jnp.bfloat16)
    own_terms = jnp.dot(masked[None, :], onehot_cands, preferred_element_type=jnp.float32)[0]
    candidate_revenue = lax.psum(own_terms, ("row", "col"))
    candidate_total = jnp.sum(candidate_revenue)
    return (owned, candidate_revenue, candidate_total)


def solution(mesh):
    in_specs = (
        P(("row", "col"), None),
        P(("row", "col")),
        P(("row", "col")),
        P(("row", "col")),
        P("col"),
        P("col"),
        P(),
    )
    out_specs = (P(("row", "col")), P(), P())
    return jax.shard_map(
        per_device, mesh=mesh, in_specs=in_specs, out_specs=out_specs, check_vma=False
    )
```

profile of v0, /device:TPU:20, one launch (start us, length us, event | category | flops | bytes accessed | tf_op | source)
XLA Modules:
  0.0 186.4 jit_solution(15897103582751986480)
XLA Ops:
  0.6 1.2 dynamic-slice
  3.2 3.9 %convert_reduce_fusion = s32[3072]{0:T(1024)S(1)} fusion(s32[3072]{0:T(1024)} %bitcast.11), kind=kLoop, calls=%fused_computation.4 | loop fusion | flops 47182848 | bytes 24576 | tf_op jit(solution)/shard_map/reduce_sum | solution.py:35
  7.0 0.7 compare_select_fusion
  7.8 0.7 add_select_fusion.1
  8.5 0.8 multiply_add_fusion
  9.3 0.9 dynamic-update-slice.1
  10.2 0.9 dynamic-update-slice
  11.0 21.6 %all-reduce.2 = (s32[88]{0:T(128)S(1)}, s32[2208]{0:T(1024)S(1)}) all-reduce(s32[88]{0:T(128)S(1)} %dynamic-update-slice.1, s32[2208]{0:T(1024)S(1)} %dynamic-update-slice), channel_id=1, replica_groups=mesh['row'=4,'col'=8] {'col'}, use_global_device_ids=true, to_apply=%add.1 | all-reduce | flops 2296 | bytes 18368
  32.6 0.3 select_reduce_fusion
  32.9 0.0 copy-start
  32.9 0.0 copy-start.1
  32.9 0.0 copy-start.2
  32.9 0.0 copy-start.4
  32.9 17.4 %gather_fusion = s32[3072]{0:T(1024)S(1)} fusion(s32[2208]{0:T(1024)S(1)} %get-tuple-element.4, s32[3072]{0:T(1024)S(1)} %get-tuple-element.8), kind=kCustom, calls=%fused_computation | custom fusion | bytes 36864 | tf_op jit(solution)/shard_map/jit(_take)/gather | solution.py:12
  50.3 0.0 copy-done
  50.4 0.0 copy-done.1
  50.4 0.0 copy-done.2
  50.4 0.0 copy-done.4
  50.4 11.8 %scatter_custom_fusion = f32[6144]{0:T(1024)S(1)} fusion(s32[3072]{0:T(1024)S(1)} %bitcast.16, f32[3072]{0:T(1024)S(1)} %get-tuple-element.5, f32[]{:T(128)} %constant.30.clone.1), kind=kCustom, calls=%fused_computation.35 | custom fusion | bytes 24580 | tf_op jit(solution)/shard_map/scatter | solution.py:38
  62.2 11.8 %scatter_custom_fusion.1 = f32[6144]{0:T(1024)S(1)} fusion(s32[3072]{0:T(1024)S(1)} %bitcast.17, f32[3072]{0:T(1024)S(1)} %get-tuple-element.9, f32[]{:T(128)} %constant.30.clone.1), kind=kCustom, calls=%fused_computation.33 | custom fusion | bytes 24580 | tf_op jit(solution)/shard_map/scatter | solution.py:43
  74.1 0.0 copy-start.5
  74.1 1.1 copy.14
  75.2 2.7 %reshape.27 = f32[4,8,384]{2,1,0:T(8,128)} reshape(f32[6144,2]{1,0:T(8,128)S(1)} %copy.14) | data formatting | bytes 98304 | tf_op jit(solution)/shard_map/reshape | solution.py:46
  77.9 4.2 %all-to-all-start = ((f32[4,8,384]{2,1,0:T(8,128)}), f32[4,8,384]{2,1,0:T(8,128)S(1)}, u32[]{:S(2)}, u32[]{:S(2)}) async-start(f32[4,8,384]{2,1,0:T(8,128)} %reshape.27), calls=%async_computation | async-start | bytes 98304 | tf_op jit(solution)/shard_map/all_to_all | solution.py:48
  82.2 3.5 %all-to-all-done = f32[4,8,384]{2,1,0:T(8,128)S(1)} async-done(((f32[4,8,384]{2,1,0:T(8,128)}), f32[4,8,384]{2,1,0:T(8,128)S(1)}, u32[]{:S(2)}, u32[]{:S(2)}) %all-to-all-start) | async-done | bytes 49184 | tf_op jit(solution)/shard_map/all_to_all | solution.py:48
  85.7 0.6 copy.15
  86.3 10.8 %all-to-all-start.1 = ((f32[4,8,384]{2,0,1:T(4,128)}), f32[4,8,384]{2,0,1:T(4,128)S(1)}, u32[]{:S(2)}, u32[]{:S(2)}) async-start(f32[4,8,384]{2,0,1:T(4,128)} %copy.15), calls=%async_computation.1 | async-start | bytes 98304 | tf_op jit(solution)/shard_map/all_to_all | solution.py:47
  97.1 0.0 copy-done.5
  97.1 2.0 %fusion.1 = f32[1,1024]{1,0:T(1,128)S(1)} fusion(bf16[3072,1]{0,1:T(2,128)(2,1)S(1)} %reshape.72, s32[1024]{0:T(1024)S(1)} %copy-done.5, s32[3072]{0:T(1024)S(1)} %get-tuple-element.7), kind=kOutput, calls=%fused_computation.7 | convolution fusion | flops 9437184 | bytes 26624 | tf_op jit(solution)/shard_map/dot_general | solution.py:60
  99.1 40.9 %psum.7 = f32[1024]{0:T(1024)S(1)} all-reduce(f32[1024]{0:T(1024)S(1)} %bitcast.19), channel_id=1, replica_groups=mesh['row'=4,'col'=8] {'row','col'}, use_global_device_ids=true, to_apply=%region_5.6 | all-reduce | flops 1024 | bytes 8192 | tf_op jit(solution)/shard_map/psum | solution.py:61
  140.0 0.0 copy-start.3
  140.0 0.6 reduce_sum.32
  140.6 0.0 all-to-all-done.1
  140.6 3.2 %reshape.28 = f32[6144,2]{1,0:T(8,128)S(1)} reshape(f32[4,8,384]{2,1,0:T(8,128)S(1)} %copy.16) | data formatting | bytes 98304 | tf_op jit(solution)/shard_map/reshape | solution.py:54
  143.7 0.9 slice_reduce_fusion
  144.6 0.0 copy-done.3
  144.6 1.7 fusion.5
  146.3 40.0 %scatter_custom_fusion.2 = f32[2048]{0:T(1024)} fusion(s32[6144]{0:T(1024)S(1)} %fusion.5, f32[6144]{0:T(1024)S(1)} %slice_reduce_fusion, f32[]{:T(128)} %constant.30.clone.1), kind=kCustom, calls=%fused_computation.43 | custom fusion | flops 6144 | bytes 8196 | tf_op jit(solution)/shard_map/scatter-add | solution.py:55
  (6 shorter events, 0.1 us)
Async XLA Ops:
  32.9 17.5 %copy-start = (s32[3072,1]{0,1:T(1,128)S(1)}, s32[3072,1]{0,1:T(1,128)}, u32[]{:S(2)}) copy-start(s32[3072,1]{0,1:T(1,128)} %param.7) | copy-start | bytes 36868
  32.9 17.5 %copy-start.1 = (s32[3072]{0:T(1024)S(1)}, s32[3072]{0:T(1024)}, u32[]{:S(2)}) copy-start(s32[3072]{0:T(1024)} %param.9) | copy-start | bytes 36868
  32.9 17.5 %copy-start.2 = (s32[3072]{0:T(1024)S(1)}, s32[3072]{0:T(1024)}, u32[]{:S(2)}) copy-start(s32[3072]{0:T(1024)} %param.8) | copy-start | bytes 36868
  32.9 17.5 %copy-start.4 = (bf16[3072]{0:T(1024)(128)(2,1)S(1)}, bf16[3072]{0:T(1024)(128)(2,1)}, u32[]{:S(2)}) copy-start(bf16[3072]{0:T(1024)(128)(2,1)} %param.10) | copy-start | bytes 18436
  74.1 23.0 %copy-start.5 = (s32[1024]{0:T(1024)S(1)}, s32[1024]{0:T(1024)}, u32[]{:S(2)}) copy-start(s32[1024]{0:T(1024)} %param.13) | copy-start | bytes 12292
  77.9 7.7 %all-to-all-start = ((f32[4,8,384]{2,1,0:T(8,128)}), f32[4,8,384]{2,1,0:T(8,128)S(1)}, u32[]{:S(2)}, u32[]{:S(2)}) async-start(f32[4,8,384]{2,1,0:T(8,128)} %reshape.27), calls=%async_computation | async-start | bytes 98304 | tf_op jit(solution)/shard_map/all_to_all | solution.py:48
  86.3 54.3 %all-to-all-start.1 = ((f32[4,8,384]{2,0,1:T(4,128)}), f32[4,8,384]{2,0,1:T(4,128)S(1)}, u32[]{:S(2)}, u32[]{:S(2)}) async-start(f32[4,8,384]{2,0,1:T(4,128)} %copy.15), calls=%async_computation.1 | async-start | bytes 98304 | tf_op jit(solution)/shard_map/all_to_all | solution.py:47
  140.0 4.7 %copy-start.3 = (f32[1024]{0:T(1024)}, f32[1024]{0:T(1024)S(1)}, u32[]{:S(2)}) copy-start(f32[1024]{0:T(1024)S(1)} %psum.7) | copy-start | bytes 12292
where the time goes:
time: 187 us; the launch traced here: 186 us
  blocking collectives  62.5 us (33%)
  local copies, waits for them, and re-layouts  52.5 us (28%)
  other arithmetic  48.8 us (26%)
  starting transfers between devices  15 us (8%)
  waiting for transfers between devices  3.5 us (2%)
  between operations  2.1 us (1%)
  matrix products  2 us (1%)
    psum x1, blocking collectives, per_device(): candidate_revenue = lax.psum(own_terms, ('row', 'col'))  40.9 us
    scatter-add x1, other arithmetic, per_device(): jax.ops.segment_sum(arrived[:, 0], arrived[:, 1].astype(jnp.int32), num_s...  40 us
    unnamed x1, blocking collectives  21.6 us
    gather x1, local copies, waits for them, and re-layouts, filtered_revenue(): supplier_word = jnp.take(supplier_all, word_index)  17.4 us
    scatter x1, local copies, waits for them, and re-layouts, per_device(): slot_offset = jnp.zeros((devices * capacity,), jnp.float32).at[slot_index...  11.8 us
    scatter x1, local copies, waits for them, and re-layouts, per_device(): jnp.zeros((devices * capacity,), jnp.float32).at[slot_index]  11.8 us
    all_to_all x1, starting transfers between devices, per_device(): lax.all_to_all(lax.all_to_all(payload, 'row', split_axis=0, concat_axis=0...  10.8 us
    all_to_all x1, starting transfers between devices, per_device(): lax.all_to_all(payload, 'row', split_axis=0, concat_axis=0, tiled=True)  4.22 us
  transfers between devices with their start and end apart: 2, of which 1 were waited for; matrix products, arithmetic and copies ran while one was open for 1% of the time, Pallas kernels for 0%

commit v1 on v0

--- a/solution.py
+++ b/solution.py
@@ -58,7 +58,8 @@
     global_id = owner * SUP_DEV + fact_offset
     onehot_cands = (global_id[:, None] == candidates[None, :]).astype(jnp.bfloat16)
     own_terms = jnp.dot(masked[None, :], onehot_cands, preferred_element_type=jnp.float32)[0]
-    candidate_revenue = lax.psum(own_terms, ("row", "col"))
+    one_axis = lax.psum(own_terms, "row")
+    candidate_revenue = lax.psum(one_axis, "col")
     candidate_total = jnp.sum(candidate_revenue)
     return (owned, candidate_revenue, candidate_total)
 

time: 187 us -> 170 us (0.909)
  the two profiles are of different devices: /device:TPU:20 before, /device:TPU:4 now
where the time goes in v1:
time: 170 us; the launch traced here: 169 us
  blocking collectives  52.9 us (31%)
  local copies, waits for them, and re-layouts  52.5 us (31%)
  other arithmetic  48.2 us (28%)
  starting transfers between devices  7.56 us (4%)
  waiting for transfers between devices  3.46 us (2%)
  between operations  2.13 us (1%)
  matrix products  2.01 us (1%)
    scatter-add x1, other arithmetic, per_device(): jax.ops.segment_sum(arrived[:, 0], arrived[:, 1].astype(jnp.int32), num_s...  39.4 us
    unnamed x1, blocking collectives  28.8 us
    gather x1, local copies, waits for them, and re-layouts, filtered_revenue(): supplier_word = jnp.take(supplier_all, word_index)  17.4 us
    psum x1, blocking collectives, per_device(): candidate_revenue = lax.psum(one_axis, 'col')  15.2 us
    scatter x1, local copies, waits for them, and re-layouts, per_device(): jnp.zeros((devices * capacity,), jnp.float32).at[slot_index]  11.8 us
    scatter x1, local copies, waits for them, and re-layouts, per_device(): slot_offset = jnp.zeros((devices * capacity,), jnp.float32).at[slot_index...  11.8 us
    psum x1, blocking collectives, per_device(): one_axis = lax.psum(own_terms, 'row')  8.9 us
    all_to_all x1, starting transfers between devices, per_device(): lax.all_to_all(payload, 'row', split_axis=0, concat_axis=0, tiled=True)  4.22 us
  transfers between devices with their start and end apart: 2, of which 1 were waited for; matrix products, arithmetic and copies ran while one was open for 2% of the time, Pallas kernels for 0%

profile of v1, /device:TPU:4, one launch (start us, length us, event | category | flops | bytes accessed | tf_op | source)
XLA Modules:
  0.0 168.8 jit_solution(12069964129701491362)
XLA Ops:
  0.6 1.2 dynamic-slice
  3.2 3.9 %convert_reduce_fusion = s32[3072]{0:T(1024)S(1)} fusion(s32[3072]{0:T(1024)} %bitcast.11), kind=kLoop, calls=%fused_computation.4 | loop fusion | flops 47182848 | bytes 24576 | tf_op jit(solution)/shard_map/reduce_sum | solution.py:35
  7.0 0.7 compare_select_fusion
  7.8 0.7 add_select_fusion.1
  8.5 0.8 multiply_add_fusion
  9.3 0.9 dynamic-update-slice.1
  10.2 0.9 dynamic-update-slice
  11.0 28.8 %all-reduce.2 = (s32[88]{0:T(128)S(1)}, s32[2208]{0:T(1024)S(1)}) all-reduce(s32[88]{0:T(128)S(1)} %dynamic-update-slice.1, s32[2208]{0:T(1024)S(1)} %dynamic-update-slice), channel_id=1, replica_groups=mesh['row'=4,'col'=8] {'col'}, use_global_device_ids=true, to_apply=%add.1 | all-reduce | flops 2296 | bytes 18368
  39.8 0.3 select_reduce_fusion
  40.1 0.0 copy-start
  40.1 0.0 copy-start.1
  40.1 0.0 copy-start.2
  40.1 0.0 copy-start.4
  40.1 17.4 %gather_fusion = s32[3072]{0:T(1024)S(1)} fusion(s32[2208]{0:T(1024)S(1)} %get-tuple-element.4, s32[3072]{0:T(1024)S(1)} %get-tuple-element.8), kind=kCustom, calls=%fused_computation | custom fusion | bytes 36864 | tf_op jit(solution)/shard_map/jit(_take)/gather | solution.py:12
  57.6 0.0 copy-done
  57.6 0.0 copy-done.1
  57.6 0.0 copy-done.2
  57.6 0.0 copy-done.4
  57.6 11.8 %scatter_custom_fusion = f32[6144]{0:T(1024)S(1)} fusion(s32[3072]{0:T(1024)S(1)} %bitcast.16, f32[3072]{0:T(1024)S(1)} %get-tuple-element.5, f32[]{:T(128)} %constant.30.clone.1), kind=kCustom, calls=%fused_computation.35 | custom fusion | bytes 24580 | tf_op jit(solution)/shard_map/scatter | solution.py:38
  69.5 11.8 %scatter_custom_fusion.1 = f32[6144]{0:T(1024)S(1)} fusion(s32[3072]{0:T(1024)S(1)} %bitcast.17, f32[3072]{0:T(1024)S(1)} %get-tuple-element.9, f32[]{:T(128)} %constant.30.clone.1), kind=kCustom, calls=%fused_computation.33 | custom fusion | bytes 24580 | tf_op jit(solution)/shard_map/scatter | solution.py:43
  81.3 0.0 copy-start.5
  81.3 1.1 copy.14
  82.4 2.7 %reshape.27 = f32[4,8,384]{2,1,0:T(8,128)} reshape(f32[6144,2]{1,0:T(8,128)S(1)} %copy.14) | data formatting | bytes 98304 | tf_op jit(solution)/shard_map/reshape | solution.py:46
  85.1 4.2 %all-to-all-start = ((f32[4,8,384]{2,1,0:T(8,128)}), f32[4,8,384]{2,1,0:T(8,128)S(1)}, u32[]{:S(2)}, u32[]{:S(2)}) async-start(f32[4,8,384]{2,1,0:T(8,128)} %reshape.27), calls=%async_computation | async-start | bytes 98304 | tf_op jit(solution)/shard_map/all_to_all | solution.py:48
  89.4 3.5 %all-to-all-done = f32[4,8,384]{2,1,0:T(8,128)S(1)} async-done(((f32[4,8,384]{2,1,0:T(8,128)}), f32[4,8,384]{2,1,0:T(8,128)S(1)}, u32[]{:S(2)}, u32[]{:S(2)}) %all-to-all-start) | async-done | bytes 49184 | tf_op jit(solution)/shard_map/all_to_all | solution.py:48
  92.8 0.6 copy.15
  93.5 3.3 %all-to-all-start.1 = ((f32[4,8,384]{2,0,1:T(4,128)}), f32[4,8,384]{2,0,1:T(4,128)S(1)}, u32[]{:S(2)}, u32[]{:S(2)}) async-start(f32[4,8,384]{2,0,1:T(4,128)} %copy.15), calls=%async_computation.1 | async-start | bytes 98304 | tf_op jit(solution)/shard_map/all_to_all | solution.py:47
  96.8 0.0 copy-done.5
  96.8 2.0 %fusion.1 = f32[1,1024]{1,0:T(1,128)S(1)} fusion(bf16[3072,1]{0,1:T(2,128)(2,1)S(1)} %reshape.72, s32[1024]{0:T(1024)S(1)} %copy-done.5, s32[3072]{0:T(1024)S(1)} %get-tuple-element.7), kind=kOutput, calls=%fused_computation.7 | convolution fusion | flops 9437184 | bytes 26624 | tf_op jit(solution)/shard_map/dot_general | solution.py:60
  98.8 8.9 %psum.14 = f32[1024]{0:T(1024)S(1)} all-reduce(f32[1024]{0:T(1024)S(1)} %bitcast.19), channel_id=1, replica_groups=mesh['row'=4,'col'=8] {'row'}, use_global_device_ids=true, to_apply=%region_5.6 | all-reduce | flops 1024 | bytes 8192 | tf_op jit(solution)/shard_map/psum | solution.py:61
  107.7 15.2 %psum.15 = f32[1024]{0:T(1024)S(1)} all-reduce(f32[1024]{0:T(1024)S(1)} %psum.14), channel_id=1, replica_groups=mesh['row'=4,'col'=8] {'col'}, use_global_device_ids=true, to_apply=%region_6.7 | all-reduce | flops 1024 | bytes 8192 | tf_op jit(solution)/shard_map/psum | solution.py:62
  122.9 0.0 copy-start.3
  123.0 0.6 reduce_sum.32
  123.6 0.0 all-to-all-done.1
  123.6 3.2 %reshape.28 = f32[6144,2]{1,0:T(8,128)S(1)} reshape(f32[4,8,384]{2,1,0:T(8,128)S(1)} %copy.16) | data formatting | bytes 98304 | tf_op jit(solution)/shard_map/reshape | solution.py:54
  126.7 0.9 slice_reduce_fusion
  127.6 0.0 copy-done.3
  127.6 1.7 %fusion.5 = s32[6144]{0:T(1024)S(1)} fusion(f32[6144,2]{1,0:T(8,128)S(1)} %reshape.28), kind=kLoop, calls=%fused_computation.13 | loop fusion | flops 6144 | bytes 49152 | tf_op jit(solution)/shard_map/convert_element_type | solution.py:56
  129.3 39.4 %scatter_custom_fusion.2 = f32[2048]{0:T(1024)} fusion(s32[6144]{0:T(1024)S(1)} %fusion.5, f32[6144]{0:T(1024)S(1)} %slice_reduce_fusion, f32[]{:T(128)} %constant.30.clone.1), kind=kCustom, calls=%fused_computation.43 | custom fusion | flops 6144 | bytes 8196 | tf_op jit(solution)/shard_map/scatter-add | solution.py:55
  (6 shorter events, 0.1 us)
Async XLA Ops:
  40.1 17.5 %copy-start = (s32[3072,1]{0,1:T(1,128)S(1)}, s32[3072,1]{0,1:T(1,128)}, u32[]{:S(2)}) copy-start(s32[3072,1]{0,1:T(1,128)} %param.7) | copy-start | bytes 36868
  40.1 17.5 %copy-start.1 = (s32[3072]{0:T(1024)S(1)}, s32[3072]{0:T(1024)}, u32[]{:S(2)}) copy-start(s32[3072]{0:T(1024)} %param.9) | copy-start | bytes 36868
  40.1 17.5 %copy-start.2 = (s32[3072]{0:T(1024)S(1)}, s32[3072]{0:T(1024)}, u32[]{:S(2)}) copy-start(s32[3072]{0:T(1024)} %param.8) | copy-start | bytes 36868
  40.1 17.5 %copy-start.4 = (bf16[3072]{0:T(1024)(128)(2,1)S(1)}, bf16[3072]{0:T(1024)(128)(2,1)}, u32[]{:S(2)}) copy-start(bf16[3072]{0:T(1024)(128)(2,1)} %param.10) | copy-start | bytes 18436
  81.3 15.5 %copy-start.5 = (s32[1024]{0:T(1024)S(1)}, s32[1024]{0:T(1024)}, u32[]{:S(2)}) copy-start(s32[1024]{0:T(1024)} %param.13) | copy-start | bytes 12292
  85.1 7.7 %all-to-all-start = ((f32[4,8,384]{2,1,0:T(8,128)}), f32[4,8,384]{2,1,0:T(8,128)S(1)}, u32[]{:S(2)}, u32[]{:S(2)}) async-start(f32[4,8,384]{2,1,0:T(8,128)} %reshape.27), calls=%async_computation | async-start | bytes 98304 | tf_op jit(solution)/shard_map/all_to_all | solution.py:48
  93.5 30.1 %all-to-all-start.1 = ((f32[4,8,384]{2,0,1:T(4,128)}), f32[4,8,384]{2,0,1:T(4,128)S(1)}, u32[]{:S(2)}, u32[]{:S(2)}) async-start(f32[4,8,384]{2,0,1:T(4,128)} %copy.15), calls=%async_computation.1 | async-start | bytes 98304 | tf_op jit(solution)/shard_map/all_to_all | solution.py:47
  122.9 4.7 %copy-start.3 = (f32[1024]{0:T(1024)}, f32[1024]{0:T(1024)S(1)}, u32[]{:S(2)}) copy-start(f32[1024]{0:T(1024)S(1)} %psum.15) | copy-start | bytes 12292
